TPU v7x, 256 devices: a whole 4x4x8 slice. The times are simulated.
256 devices in a mesh: dp: 16 (over z, y_hi), blk: 16 (over y_lo, x, core).
Axes of the slice: x: 4, y: 4 (y_hi: 2, y_lo: 2; y = y_hi * 2 + y_lo), z: 8, core: 2. Of those that a mesh axis runs over, the one named last changes fastest.
Arguments:
- q_raw: bfloat16 [16, 2048, 1536], P('dp', 'blk'), may hold values from -120 to 120
- q_tan: bfloat16 [16, 2048, 1536], P('dp', 'blk'), may hold values from -6 to 6
- k_raw: bfloat16 [16, 2048, 1536], P('dp', 'blk'), may hold values from -120 to 120
- k_tan: bfloat16 [16, 2048, 1536], P('dp', 'blk'), may hold values from -6 to 6
- values: bfloat16 [16, 2048, 1536], P('dp', 'blk'), may hold values from -6 to 6
- values_tan: bfloat16 [16, 2048, 1536], P('dp', 'blk'), may hold values from -6 to 6
- head_scale: float32 [12], replicated, may hold values from 1 to 3
- w_out: bfloat16 [1536, 1536], P('dp'), may hold values from -0.15625 to 0.15625
- gate: float32 [16, 1536], P('dp'), may hold values from 0.5 to 1.5
- gate_tan: float32 [16, 1536], P('dp'), may hold values from -4 to 4
Outputs:
- layer_out: bfloat16 [16, 2048, 1536], P('dp', 'blk')
- layer_tan: bfloat16 [16, 2048, 1536], P('dp', 'blk')
All inputs are finite; a program needn't handle non-finite values.
Results may differ from a plain program's by a relative error of at most 0.012.
Values may be sent and summed in bfloat16 or wider, within the bound.
A program may use at most 128 MiB of HBM per device.

v0:
```python
import math

import jax
import jax.numpy as jnp
from jax import lax
from jax.sharding import PartitionSpec as P

HEADS = 12
HEAD = 128
HD = 1536


epsilon = 1e-06


def normalize(raw_rows, tan_rows):
    shape = raw_rows.shape[:-1] + (HEADS, HEAD)
    direct = raw_rows.astype(jnp.float32).reshape(shape)
    moving = tan_rows.astype(jnp.float32).reshape(shape)
    recip = lax.rsqrt(jnp.mean(direct * direct, -1, keepdims=True) + epsilon)
    normed = direct * recip
    normed_tan = recip * (moving - normed * jnp.mean(normed * moving, -1, keepdims=True))
    return (normed.astype(jnp.bfloat16), normed_tan.astype(jnp.bfloat16))


def score_pair(q_norm, q_pair, key_flat, key_tan_flat, score_scale):
    count = key_flat.shape[0]
    key_norm = key_flat.reshape(count, HEADS, HEAD)
    key_pair = jnp.concatenate([key_norm, key_tan_flat.reshape(count, HEADS, HEAD)], -1)
    scores = (
        jnp.einsum("qhe,khe->qhk", q_norm, key_norm, preferred_element_type=jnp.float32)
        * score_scale
    )
    slopes = (
        jnp.einsum("qhe,khe->qhk", q_pair, key_pair, preferred_element_type=jnp.float32)
        * score_scale
    )
    return (scores, slopes)


def shards(q_raw, q_tan, k_raw, k_tan, values, values_tan, head_scale, w_out, gate, gate_tan):
    rows = q_raw.shape[1]
    q_norm, q_dir = normalize(q_raw[0], q_tan[0])
    k_norm, k_dir = normalize(k_raw[0], k_tan[0])
    key_flat = k_norm.reshape(rows, HD)
    key_tan_flat = k_dir.reshape(rows, HD)
    val_flat = values[0]
    val_tan_flat = values_tan[0]
    score_scale = (head_scale / math.sqrt(HEAD))[None, :, None]
    q_pair = jnp.concatenate([q_dir, q_norm], -1)
    all_keys, all_vals = (
        lax.all_gather(key_flat, "blk", axis=0, tiled=True),
        lax.all_gather(val_flat, "blk", axis=0, tiled=True),
    )
    whole_count = all_keys.shape[0]
    all_scores = (
        jnp.einsum(
            "qhe,khe->qhk",
            q_norm,
            all_keys.reshape(whole_count, HEADS, HEAD),
            preferred_element_type=jnp.float32,
        )
        * score_scale
    )
    all_probs = jnp.exp(all_scores)
    totals = jnp.sum(all_probs, -1)
    mixed = jnp.einsum(
        "qhk,khe->qhe",
        all_probs.astype(jnp.bfloat16),
        all_vals.reshape(whole_count, HEADS, HEAD),
        preferred_element_type=jnp.float32,
    )
    pieces = (
        lax.all_gather(key_tan_flat, "blk", axis=0, tiled=True),
        lax.all_gather(val_tan_flat, "blk", axis=0, tiled=True),
    )
    count = pieces[0].shape[0]
    val_part = all_vals.reshape(count, HEADS, HEAD)
    scores, slopes = score_pair(q_norm, q_pair, all_keys, pieces[0], score_scale)
    probs = jnp.exp(scores)
    prob_half = probs.astype(jnp.bfloat16)
    slope_half = (probs * slopes).astype(jnp.bfloat16)
    val_tan = pieces[1].reshape(count, HEADS, HEAD)
    more_tan = jnp.einsum("qhk,khe->qhe", slope_half, val_part, preferred_element_type=jnp.float32)
    more_tan = more_tan + jnp.einsum(
        "qhk,khe->qhe", prob_half, val_tan, preferred_element_type=jnp.float32
    )
    moments = jnp.sum(probs * slopes, -1)
    attended = (mixed / totals[..., None]).astype(jnp.bfloat16).reshape(rows, HD)
    attended_tan = (
        more_tan / totals[..., None] - mixed * moments[..., None] / (totals * totals)[..., None]
    )
    attended_tan = attended_tan.astype(jnp.bfloat16).reshape(rows, HD)
    stacked = jnp.concatenate([attended, attended_tan], 0)
    projected = jnp.dot(
        stacked, lax.all_gather(w_out, "dp", axis=0, tiled=True), preferred_element_type=jnp.float32
    )
    gate_row = gate[0][None, :]
    gate_tan_row = gate_tan[0][None, :]
    layer_out = (gate_row * projected[:rows]).astype(jnp.bfloat16)
    layer_tan = (gate_tan_row * projected[:rows] + gate_row * projected[rows:]).astype(jnp.bfloat16)
    return (layer_out[None], layer_tan[None])


def solution(mesh):
    return jax.shard_map(
        shards,
        mesh=mesh,
        in_specs=(
            P("dp", "blk", None),
            P("dp", "blk", None),
            P("dp", "blk", None),
            P("dp", "blk", None),
            P("dp", "blk", None),
            P("dp", "blk", None),
            P(),
            P("dp", None),
            P("dp", None),
            P("dp", None),
        ),
        out_specs=(P("dp", "blk", None), P("dp", "blk", None)),
        check_vma=False,
    )
```

profile of v0, /device:TPU:1, one launch (start us, length us, event | category | flops | bytes accessed | tf_op | source)
XLA Modules:
  0.0 337.2 jit_solution(3919737039438799846)
XLA Ops:
  7.2 0.0 copy-start
  7.2 0.0 copy-start.1
  7.2 0.0 copy-start.2
  7.2 0.0 copy-start.3
  7.2 0.0 all-gather.8.cloned.1.call-start
  7.3 1.3 copy.19
  8.5 0.0 copy-start.4
  8.5 0.1 multiply_reduce_fusion.3
  8.7 1.2 copy.25
  9.9 0.1 multiply_reduce_fusion.1
  10.0 1.1 fusion.23
  11.1 0.0 all-gather.8.cloned.1.call-update
  11.1 0.0 all-gather.10.cloned.1.call-start
  11.2 0.7 all-gather.10.cloned.1.call-update
  11.9 0.0 all-gather.14.cloned.1.call-start
  11.9 0.7 all-gather.14.cloned.1.call-update
  12.6 0.0 all-gather.16.cloned.1.call-start
  12.7 0.5 all-gather.16.cloned.1.call-update
  13.2 0.0 all-gather.12.cloned.1.call-start
  13.2 0.5 all-gather.12.cloned.1.call-update
  13.8 0.0 copy-done
  13.8 0.2 copy.20
  14.0 0.2 copy.21
  14.2 0.0 copy-done.1
  14.2 0.2 copy.28
  14.4 0.2 copy.30
  14.6 0.0 copy-done.2
  14.7 0.1 multiply_reduce_fusion.2
  14.8 0.5 multiply_reduce_fusion
  15.4 0.5 multiply_convert_fusion.1
  15.9 54.0 %all-gather.8.cloned.1.call-done = bf16[2048,1536]{0,1:T(8,128)(2,1)} async-done(((bf16[128,1536]{0,1:T(8,128)(2,1)}), bf16[2048,1536]{0,1:T(8,128)(2,1)}) %all-gather.8.cloned.1.call-update) | async-done | bytes 6291472 | tf_op jit(solution)/shard_map/all_gather | solution.py:52
  69.9 8.7 %copy.26 = bf16[2048,12,128]{2,0,1:T(8,128)(2,1)} copy(bf16[2048,12,128]{0,2,1:T(8,128)(2,1)} %bitcast.68) | data formatting | bytes 12582912 | tf_op jit(solution)/shard_map/reshape | solution.py:60
  78.6 48.6 %all-gather.10.cloned.1.call-done = bf16[2048,1536]{0,1:T(8,128)(2,1)} async-done(((bf16[128,1536]{0,1:T(8,128)(2,1)}), bf16[2048,1536]{0,1:T(8,128)(2,1)}) %all-gather.10.cloned.1.call-update) | async-done | bytes 6291472 | tf_op jit(solution)/shard_map/all_gather | solution.py:74
  127.2 8.6 %copy.27 = bf16[2048,12,128]{2,0,1:T(8,128)(2,1)} copy(bf16[2048,12,128]{0,2,1:T(8,128)(2,1)} %bitcast.75) | data formatting | bytes 12582912 | tf_op jit(solution)/shard_map/reshape | solution.py:29
  135.8 10.8 %bitcast_reduce_fusion = (f32[128,12]{0,1:T(8,128)S(1)}, f32[12,2048,128]{2,1,0:T(8,128)}) fusion(f32[12]{0:T(128)S(1)} %broadcast_multiply_fusion.2, bf16[2048,12,128]{0,2,1:T(8,128)(2,1)} %bitcast.69, bf16[128,12,128]{2,0,1:T(8,128)(2,1)S(1)} %get-tuple-element.7), kind=kOutput, calls=%fused_computation.5 | convolution fusion | flops 811596288 | bytes 19273776 | tf_op jit(solution)/shard_map/qhe,khe->qhk/dot_general | solution.py:57
  146.6 27.9 %all-gather.14.cloned.1.call-done = bf16[1,2048,1536]{2,1,0:T(8,128)(2,1)} async-done(((bf16[1,128,1536]{2,1,0:T(8,128)(2,1)}), bf16[1,2048,1536]{2,1,0:T(8,128)(2,1)}) %all-gather.14.cloned.1.call-update) | async-done | bytes 6291472 | tf_op jit(solution)/shard_map/all_gather | solution.py:53
  174.5 8.6 %copy.23 = bf16[1,2048,1536]{1,2,0:T(8,128)(2,1)} copy(bf16[1,2048,1536]{2,1,0:T(8,128)(2,1)} %all-gather.14.cloned.1.call-done) | data formatting | bytes 12582912 | tf_op jit(solution)/shard_map/all_gather | solution.py:53
  183.1 38.8 %all-gather.16.cloned.1.call-done = bf16[1,2048,1536]{2,1,0:T(8,128)(2,1)} async-done(((bf16[1,128,1536]{2,1,0:T(8,128)(2,1)}), bf16[1,2048,1536]{2,1,0:T(8,128)(2,1)}) %all-gather.16.cloned.1.call-update) | async-done | bytes 6291472 | tf_op jit(solution)/shard_map/all_gather | solution.py:75
  221.9 8.9 %copy.32 = bf16[1,2048,1536]{1,2,0:T(8,128)(2,1)} copy(bf16[1,2048,1536]{2,1,0:T(8,128)(2,1)} %all-gather.16.cloned.1.call-done) | data formatting | bytes 12582912 | tf_op jit(solution)/shard_map/all_gather | solution.py:75
  230.9 9.2 %fusion.39 = f32[12,128,128]{1,2,0:T(8,128)S(1)} fusion(bf16[2048,12,128]{0,2,1:T(8,128)(2,1)} %bitcast.74, f32[12,2048,128]{2,1,0:T(8,128)} %get-tuple-element.11, f32[12]{0:T(128)S(1)} %broadcast_multiply_fusion.2), kind=kOutput, calls=%fused_computation.49 | convolution fusion | flops 811597824 | bytes 19660848 | tf_op jit(solution)/shard_map/qhk,khe->qhe/dot_general | solution.py:85
  240.1 0.0 slice-done
  240.1 0.0 slice-done.1
  240.1 7.3 %divide_convert_fusion = (bf16[128,12,128]{0,2,1:T(8,128)(2,1)S(1)}, f32[128,12,128]{0,2,1:T(8,128)S(1)}) fusion(f32[128,12]{0,1:T(8,128)S(1)} %get-tuple-element.10, bf16[2048,12,128]{0,2,1:T(8,128)(2,1)S(1)} %bitcast.72, f32[12,2048,128]{2,1,0:T(8,128)} %get-tuple-element.11, f32[12]{0:T(128)S(1)} %broadcast_multiply_fusion.2), kind=kOutput, calls=%fused_computation.35 | convolution fusion | flops 811991040 | bytes 20060208 | tf_op jit(solution)/shard_map/qhk,khe->qhe/dot_general | solution.py:67
  247.4 13.0 %fusion.40 = (f32[128,12]{0,1:T(8,128)S(1)}, bf16[128,12,2048]{0,2,1:T(8,128)(2,1)}) fusion(bf16[128,12,128]{2,0,1:T(8,128)(2,1)S(1)} %get-tuple-element.7, bf16[128,12,128]{2,0,1:T(8,128)(2,1)S(1)} %get-tuple-element.6, bf16[2048,12,128]{2,0,1:T(8,128)(2,1)} %copy.27, bf16[2048,12,128]{2,0,1:T(8,128)(2,1)} %copy.26, ...), kind=kOutput, calls=%fused_computation.50 | convolution fusion | flops 1653078528 | bytes 32249904 | tf_op jit(solution)/shard_map/qhe,khe->qhk/dot_general | solution.py:35
  260.4 4.6 %fusion.20 = bf16[128,12,128]{0,2,1:T(8,128)(2,1)S(1)} fusion(f32[12,128,128]{1,2,0:T(8,128)S(1)} %fusion.39, bf16[2048,12,128]{0,2,1:T(8,128)(2,1)S(1)} %bitcast.73, bf16[128,12,2048]{0,2,1:T(8,128)(2,1)} %get-tuple-element.13, f32[128,12,128]{0,2,1:T(8,128)S(1)} %get-tuple-element.15, f32[128,12]{0,1:T(8,128)S(1)} %mul.183, ...), kind=kOutput, calls=%fused_computation.17 | convolution fusion | flops 806486016 | bytes 14567424 | tf_op jit(solution)/shard_map/qhk,khe->qhe/dot_general | solution.py:84
  265.0 60.8 %all-gather.12.cloned.1.call-done = bf16[1536,1536]{1,0:T(8,128)(2,1)} async-done(((bf16[96,1536]{1,0:T(8,128)(2,1)}), bf16[1536,1536]{1,0:T(8,128)(2,1)}) %all-gather.12.cloned.1.call-update) | async-done | bytes 4718608 | tf_op jit(solution)/shard_map/all_gather | solution.py:96
  325.9 3.7 %fusion.29 = f32[256,1536]{1,0:T(8,128)S(1)} fusion(bf16[1536,1536]{1,0:T(8,128)(2,1)} %all-gather.12.cloned.1.call-done, bf16[128,1536]{0,1:T(8,128)(2,1)S(1)} %bitcast.82, bf16[128,1536]{0,1:T(8,128)(2,1)S(1)} %bitcast.81), kind=kOutput, calls=%fused_computation.25 | convolution fusion | flops 1209532416 | bytes 7077888 | tf_op jit(solution)/shard_map/dot_general | solution.py:95
  329.6 1.0 fusion.36
  (13 shorter events, 0.1 us)
Async XLA Ops:
  7.2 6.6 %copy-start = (bf16[1,128,1536]{2,1,0:T(8,128)(2,1)S(1)}, bf16[1,128,1536]{2,1,0:T(8,128)(2,1)}, u32[]{:S(2)}) copy-start(bf16[1,128,1536]{2,1,0:T(8,128)(2,1)} %param.10) | copy-start | bytes 1179652
  7.2 7.0 %copy-start.1 = (bf16[1,128,1536]{2,1,0:T(8,128)(2,1)S(1)}, bf16[1,128,1536]{2,1,0:T(8,128)(2,1)}, u32[]{:S(2)}) copy-start(bf16[1,128,1536]{2,1,0:T(8,128)(2,1)} %param.11) | copy-start | bytes 1179652
  7.2 7.5 %copy-start.2 = (f32[1,1536]{1,0:T(1,128)S(1)}, f32[1,1536]{1,0:T(1,128)}, u32[]{:S(2)}) copy-start(f32[1,1536]{1,0:T(1,128)} %param.18) | copy-start | bytes 18436
  7.2 7.5 %copy-start.3 = (f32[1,1536]{1,0:T(1,128)S(1)}, f32[1,1536]{1,0:T(1,128)}, u32[]{:S(2)}) copy-start(f32[1,1536]{1,0:T(1,128)} %param.19) | copy-start | bytes 18436
  7.2 62.7 %all-gather.8.cloned.1.call-start = ((), (), s32[]{:S(2)}) async-start(), calls=%async_computation | async-start | bytes 6684672 | tf_op jit(solution)/shard_map/all_gather | solution.py:52
  8.5 6.8 %copy-start.4 = (f32[12]{0:T(128)S(1)}, f32[12]{0:T(128)}, u32[]{:S(2)}) copy-start(f32[12]{0:T(128)} %param.16) | copy-start | bytes 148
  11.1 116.0 %all-gather.10.cloned.1.call-start = ((), (), s32[]{:S(2)}) async-start(), calls=%async_computation.1 | async-start | bytes 6684672 | tf_op jit(solution)/shard_map/all_gather | solution.py:74
  11.9 162.6 %all-gather.14.cloned.1.call-start = ((), (), s32[]{:S(2)}) async-start(), calls=%async_computation.3 | async-start | bytes 6684672 | tf_op jit(solution)/shard_map/all_gather | solution.py:53
  12.6 209.3 %all-gather.16.cloned.1.call-start = ((), (), s32[]{:S(2)}) async-start(), calls=%async_computation.4 | async-start | bytes 6684672 | tf_op jit(solution)/shard_map/all_gather | solution.py:75
  13.2 312.7 %all-gather.12.cloned.1.call-start = ((), (), s32[]{:S(2)}) async-start(), calls=%async_computation.2 | async-start | bytes 5013504 | tf_op jit(solution)/shard_map/all_gather | solution.py:96
  221.9 18.1 %slice-start = ((s8[6291456]{0:T(1024)(128)(4,1)}), s8[2097152]{0:T(1024)(128)(4,1)S(1)}, s32[]{:S(2)}) async-start(s8[6291456]{0:T(1024)(128)(4,1)} %bitcast.70), calls=%async_computation.5 | async-start | bytes 4194304
  230.8 9.2 %slice-start.1 = ((s8[6291456]{0:T(1024)(128)(4,1)}), s8[4194304]{0:T(1024)(128)(4,1)S(1)}, s32[]{:S(2)}) async-start(s8[6291456]{0:T(1024)(128)(4,1)} %bitcast.70), calls=%async_computation.6 | async-start | bytes 8388608
Sparse Core Ops, SparseCore 0:
  11.3 58.5 all-gather.7
  72.2 54.9 all-gather.9
  129.0 45.4 all-gather.13
  176.2 45.6 all-gather.15
  224.4 101.4 all-gather.11
where the time goes:
time: 341 us; the launch traced here: 337 us
  waiting for transfers between devices  233 us (68%)
  matrix products  48.6 us (14%)
  local copies, waits for them, and re-layouts  38.1 us (11%)
  between operations  14 us (4%)
  other arithmetic  3.49 us (1%)
    all_gather x1, waiting for transfers between devices, shards(): lax.all_gather(w_out, 'dp', axis=0, tiled=True)  60.8 us
    all_gather x1, waiting for transfers between devices, shards(): lax.all_gather(key_flat, 'blk', axis=0, tiled=True)  54 us
    all_gather x1, waiting for transfers between devices, shards(): lax.all_gather(key_tan_flat, 'blk', axis=0, tiled=True)  48.6 us
    all_gather x1, waiting for transfers between devices, shards(): lax.all_gather(val_tan_flat, 'blk', axis=0, tiled=True)  38.8 us
    all_gather x1, waiting for transfers between devices, shards(): lax.all_gather(val_flat, 'blk', axis=0, tiled=True)  27.9 us
    dot_general x1, matrix products, score_pair(): jnp.einsum('qhe,khe->qhk', q_pair, key_pair, preferred_element_type=jnp.f...  13 us
    dot_general x1, matrix products, shards(): jnp.einsum('qhe,khe->qhk', q_norm, all_keys.reshape(whole_count, HEADS, H...  10.8 us
    dot_general x1, matrix products, shards(): jnp.einsum('qhk,khe->qhe', prob_half, val_tan, preferred_element_type=jnp...  9.2 us
  transfers between devices with their start and end apart: 5, of which 5 were waited for; matrix products, arithmetic and copies ran while one was open for 24% of the time, Pallas kernels for 0%

commit v1 on v0

v1 whole, which is shorter than its diff:
```python
import math

import jax
import jax.numpy as jnp
from jax import lax
from jax.experimental import pallas as pl
from jax.experimental.pallas import tpu as pltpu
from jax.sharding import PartitionSpec as P

HEADS = 12
HEAD = 128
HD = 1536
ROWS = 128
NX = 4
PER = 3
KEYS = 512
CHUNK = 256
DP_ROWS = 96
HALF = 768
MESH = pl.DeviceIdType.MESH
NT = (((1,), (1,)), ((), ()))
ORDER = (0, 1, 3, 2)
AHEAD = 3

epsilon = 1e-06


def unit_rows(x, dx):
    recip = lax.rsqrt(jnp.mean(x * x, -1, keepdims=True) + epsilon)
    normed = x * recip
    moved = recip * (dx - normed * jnp.mean(normed * dx, -1, keepdims=True))
    return normed.astype(jnp.bfloat16), moved.astype(jnp.bfloat16)


def body(
    q_hbm, qt_hbm, k_hbm, kt_hbm, v_hbm, vt_hbm, scale_ref, w_hbm, out_ref,
    raw, kv, kv_send, qb, q_send, pv, uv, tot, mom, ret, att, w_mine, w_other,
    load_sem, xs, xr, qs, qr, ys, yr, cs, cr, ds, dr, rs, rr,
    w_load, os, orr, ps, pr, ms, mr, ws, wr,
):
    blk, dp = lax.axis_index("blk"), lax.axis_index("dp")
    y, x, c = blk // 8, (blk // 2) % NX, blk % 2
    z, yh = dp // 2, dp % 2

    def at_x(j):
        return {"dp": dp, "blk": y * 8 + ((x + j) % NX) * 2 + c}

    y_peer = {"dp": dp, "blk": (1 - y) * 8 + x * 2 + c}
    c_peer = {"dp": dp, "blk": y * 8 + x * 2 + (1 - c)}
    outer = {"dp": z * 2 + (1 - yh), "blk": (1 - y) * 8 + x * 2 + c}
    z_up = {"dp": ((z + 1) % 8) * 2 + yh, "blk": blk}
    z_down = {"dp": ((z + 7) % 8) * 2 + yh, "blk": blk}

    barrier = pltpu.get_barrier_semaphore()
    peers = [at_x(1), at_x(2), at_x(3), y_peer, c_peer, outer, z_up, z_down]
    for peer in peers:
        pl.semaphore_signal(barrier, inc=1, device_id=peer, device_id_type=MESH)
    loads = []
    for n, src in enumerate((k_hbm, kt_hbm, v_hbm, vt_hbm, q_hbm, qt_hbm)):
        copy = pltpu.make_async_copy(src.at[0], raw.at[n], load_sem.at[n])
        copy.start()
        loads.append(copy)
    my_rows = pl.ds(pl.multiple_of(dp * DP_ROWS, DP_ROWS), DP_ROWS)
    my_cols = pl.ds(pl.multiple_of(c * HALF, HALF), HALF)
    w_copy = pltpu.make_async_copy(w_hbm.at[:, my_cols], w_mine.at[my_rows], w_load)
    w_copy.start()
    pl.semaphore_wait(barrier, len(peers))

    sent = []

    def remote(src, dst, send_sem, recv_sem, peer):
        copy = pltpu.make_async_remote_copy(
            src_ref=src, dst_ref=dst, send_sem=send_sem, recv_sem=recv_sem,
            device_id=peer, device_id_type=MESH,
        )
        copy.start()
        sent.append(copy)
        return copy

    x_in, q_in, y_in, c_in, d_in, r_in = {}, {}, {}, {}, {}, {}

    def forward(i, j):
        own = kv.at[i, j, pl.ds(0, ROWS)]
        y_in[i, j] = remote(own, kv.at[i, j, pl.ds(ROWS, ROWS)], ys.at[i, j], yr.at[i, j], y_peer)
        c_in[i, j] = remote(own, kv.at[i, j, pl.ds(2 * ROWS, ROWS)], cs.at[i, j], cr.at[i, j], c_peer)

    def relay(i, j):
        y_in[i, j].wait_recv()
        d_in[i, j] = remote(
            kv.at[i, j, pl.ds(ROWS, ROWS)], kv.at[i, j, pl.ds(3 * ROWS, ROWS)],
            ds.at[i, j], dr.at[i, j], c_peer,
        )

    def columns(i, j):
        head = PER * ((x + j) % NX) + i
        return pl.ds(pl.multiple_of(head * HEAD, HEAD), HEAD)

    def send_keys(i, j):
        cols = columns(i, j)
        normed, moved = unit_rows(
            raw[0, :, cols].astype(jnp.float32), raw[1, :, cols].astype(jnp.float32)
        )
        dst = kv.at[i, 0, pl.ds(0, ROWS)] if j == 0 else kv_send.at[i, j - 1]
        dst[:, 0:128] = normed
        dst[:, 128:256] = moved
        dst[:, 256:384] = raw[2, :, cols]
        dst[:, 384:512] = raw[3, :, cols]
        if j == 0:
            forward(i, 0)
        else:
            x_in[i, j] = remote(
                dst, kv.at[i, j, pl.ds(0, ROWS)], xs.at[i, j], xr.at[i, j], at_x(j)
            )

    def send_queries(i, j):
        cols = columns(i, j)
        normed, moved = unit_rows(
            raw[4, :, cols].astype(jnp.float32), raw[5, :, cols].astype(jnp.float32)
        )
        dst = qb.at[i, pl.ds(0, ROWS)] if j == 0 else q_send.at[i, j - 1]
        dst[:, 0:128] = moved
        dst[:, 128:256] = normed
        if j != 0:
            q_in[i, j] = remote(
                dst, qb.at[i, pl.ds(j * ROWS, ROWS)], qs.at[i, j], qr.at[i, j], at_x(j)
            )

    w_copy.wait()
    outer_in = remote(w_mine.at[my_rows], w_mine.at[my_rows], os, orr, outer)

    for n in range(4):
        loads[n].wait()
    for j in ORDER:
        send_keys(0, j)
    loads[4].wait()
    loads[5].wait()
    for j in ORDER:
        send_queries(0, j)

    def w_block(step):
        block = (z + step + 8) % 8
        return pl.ds(pl.multiple_of(block * 192, 192), 192)

    w_in = []
    up_in, down_in = {}, {}

    def w_pass(step):
        if step == 0:
            outer_in.wait_recv()
        else:
            up_in[step].wait_recv()
            if step <= 3:
                down_in[step].wait_recv()
        low = w_block(-step)
        if step < 4:
            up_in[step + 1] = remote(
                w_mine.at[low], w_mine.at[low], ps.at[step], pr.at[step], z_up
            )
        w_in.append(remote(w_mine.at[low], w_other.at[low], ws.at[step], wr.at[step], c_peer))
        if step <= 3:
            high = w_block(step)
            if step < 3:
                down_in[step + 1] = remote(
                    w_mine.at[high], w_mine.at[high], ms.at[step], mr.at[step], z_down
                )
            if step > 0:
                w_in.append(
                    remote(w_mine.at[high], w_other.at[high], ws.at[4 + step], wr.at[4 + step], c_peer)
                )

    w_pass(0)
    for i in range(1, PER):
        for j in ORDER:
            send_keys(i, j)
        for j in ORDER:
            send_queries(i, j)

    steps = [(i, j) for i in range(PER) for j in ORDER]
    passed = 0

    def pass_up_to(n):
        nonlocal passed
        while passed < min(n, len(steps)):
            i, j = steps[passed]
            if j != 0:
                x_in[i, j].wait_recv()
                forward(i, j)
            passed += 1

    def attend(i, j):
        scale = scale_ref[PER * x + i] * (1.0 / math.sqrt(HEAD))
        rate = scale * math.log2(math.e)

        def chunk(n, carry):
            rows = pl.ds(pl.multiple_of(n * CHUNK, CHUNK), CHUNK)
            queries = qb[i, rows, :]
            scores = lax.dot_general(
                queries[:, 128:256], kv[i, j, :, 0:128], NT, preferred_element_type=jnp.float32
            )
            slopes = lax.dot_general(
                queries, kv[i, j, :, 0:256], NT, preferred_element_type=jnp.float32
            )
            probs = jnp.exp2(scores * rate)
            weighted = probs * (slopes * scale)
            p_sum = probs[:, 0:128]
            w_sum = weighted[:, 0:128]
            for part in range(1, KEYS // 128):
                p_sum = p_sum + probs[:, part * 128 : (part + 1) * 128]
                w_sum = w_sum + weighted[:, part * 128 : (part + 1) * 128]
            p_mix = jnp.dot(
                probs.astype(jnp.bfloat16), kv[i, j, :, 256:512], preferred_element_type=jnp.float32
            )
            w_mix = jnp.dot(
                weighted.astype(jnp.bfloat16), kv[i, j, :, 256:384], preferred_element_type=jnp.float32
            )
            if j == 0:
                tot[rows, :] = p_sum
                mom[rows, :] = w_sum
                pv[rows, :] = p_mix
                uv[rows, :] = w_mix
            else:
                tot[rows, :] += p_sum
                mom[rows, :] += w_sum
                pv[rows, :] += p_mix
                uv[rows, :] += w_mix
            return carry

        lax.fori_loop(0, KEYS // CHUNK, chunk, 0)

    def finish(i):
        head = PER * x + i
        cols = pl.ds(pl.multiple_of(head * HEAD, HEAD), HEAD)
        for j in (2, 1, 3, 0):
            rows = pl.ds(j * ROWS, ROWS)
            inv = 1.0 / jnp.sum(tot[rows, :], -1, keepdims=True)
            moment = jnp.sum(mom[rows, :], -1, keepdims=True) * inv
            mixed = pv[rows, 0:128]
            main = (mixed * inv).astype(jnp.bfloat16)
            tangent = ((uv[rows, :] + pv[rows, 128:256] - mixed * moment) * inv).astype(jnp.bfloat16)
            if j == 0:
                att[0:ROWS, cols] = main
                att[ROWS : 2 * ROWS, cols] = tangent
            else:
                ret[i, j - 1, 0:ROWS, :] = main
                ret[i, j - 1, ROWS : 2 * ROWS, :] = tangent
                r_in[i, j] = remote(
                    ret.at[i, j - 1], att.at[:, cols], rs.at[i, j], rr.at[i, j], at_x(NX - j)
                )

    w_steps = {3: 1, 5: 2, 8: 3, 10: 4}
    pass_up_to(AHEAD)
    relay(*steps[0])
    for n, (i, j) in enumerate(steps):
        pass_up_to(n + 1 + AHEAD)
        if n in w_steps:
            w_pass(w_steps[n])
        if n + 1 < len(steps):
            relay(*steps[n + 1])
        if j == 0:
            for other in ORDER[1:]:
                q_in[i, other].wait_recv()
        c_in[i, j].wait_recv()
        d_in[i, j].wait_recv()
        attend(i, j)
        if j == ORDER[-1]:
            finish(i)

    for copy in w_in:
        copy.wait_recv()
    for copy in r_in.values():
        copy.wait_recv()

    def project(n, carry):
        for half, offset in ((w_mine, c), (w_other, 1 - c)):
            cols = pl.ds(pl.multiple_of(offset * HALF + n * 256, 256), 256)
            out_ref[:, cols] = jnp.dot(
                att[...], half[:, pl.ds(pl.multiple_of(n * 256, 256), 256)],
                preferred_element_type=jnp.float32,
            )
        return carry

    lax.fori_loop(0, HALF // 256, project, 0)
    for copy in sent:
        copy.wait_send()


def attention(q_raw, q_tan, k_raw, k_tan, values, values_tan, head_scale, w_out):
    bf16, f32 = jnp.bfloat16, jnp.float32
    dma = pltpu.SemaphoreType.DMA
    any_spec = pl.BlockSpec(memory_space=pl.ANY)
    return pl.pallas_call(
        body,
        out_shape=jax.ShapeDtypeStruct((2 * ROWS, HD), f32),
        in_specs=[any_spec] * 6 + [pl.BlockSpec(memory_space=pltpu.SMEM), any_spec],
        out_specs=pl.BlockSpec(memory_space=pltpu.VMEM),
        scratch_shapes=[
            pltpu.VMEM((6, ROWS, HD), bf16),
            pltpu.VMEM((PER, NX, KEYS, 512), bf16),
            pltpu.VMEM((PER, NX - 1, ROWS, 512), bf16),
            pltpu.VMEM((PER, KEYS, 256), bf16),
            pltpu.VMEM((PER, NX - 1, ROWS, 256), bf16),
            pltpu.VMEM((KEYS, 256), f32),
            pltpu.VMEM((KEYS, 128), f32),
            pltpu.VMEM((KEYS, 128), f32),
            pltpu.VMEM((KEYS, 128), f32),
            pltpu.VMEM((PER, NX - 1, 2 * ROWS, HEAD), bf16),
            pltpu.VMEM((2 * ROWS, HD), bf16),
            pltpu.VMEM((HD, HALF), bf16),
            pltpu.VMEM((HD, HALF), bf16),
            dma((6,)),
        ]
        + [dma((PER, NX))] * 12
        + [dma, dma, dma]
        + [dma((4,)), dma((4,)), dma((3,)), dma((3,)), dma((8,)), dma((8,))],
        compiler_params=pltpu.CompilerParams(
            collective_id=0, has_side_effects=True, vmem_limit_bytes=48 * 1024 * 1024
        ),
        cost_estimate=pl.CostEstimate(
            flops=7_000_000_000, bytes_accessed=10_000_000, transcendentals=3_200_000
        ),
        name="attention",
    )(q_raw, q_tan, k_raw, k_tan, values, values_tan, head_scale, w_out)


def shards(q_raw, q_tan, k_raw, k_tan, values, values_tan, head_scale, w_out, gate, gate_tan):
    projected = attention(q_raw, q_tan, k_raw, k_tan, values, values_tan, head_scale, w_out)
    layer_out = (gate * projected[:ROWS]).astype(jnp.bfloat16)
    layer_tan = (gate_tan * projected[:ROWS] + gate * projected[ROWS:]).astype(jnp.bfloat16)
    return (layer_out[None], layer_tan[None])


def solution(mesh):
    rows = P("dp", "blk", None)
    return jax.shard_map(
        shards,
        mesh=mesh,
        in_specs=(rows,) * 6 + (P(), P("dp", None), P("dp", None), P("dp", None)),
        out_specs=(rows, rows),
        check_vma=False,
    )
```

time: 341 us -> 77.9 us (0.23)
  waiting for transfers between devices: 233 us -> 0 us
  Pallas kernels: 0 us -> 66.7 us
  matrix products: 48.6 us -> 0 us
  local copies, waits for them, and re-layouts: 38.1 us -> 7.58 us
  between operations: 14 us -> 0.66 us
    all_gather x5 -> x0, waiting for transfers between devices: 230 us -> none  [the longest x1 60.8 us: shards(): lax.all_gather(w_out, 'dp', axis=0, tiled=True)]
    pallas_call x0 -> x1, Pallas kernels: none -> 66.7 us  [attention(): pl.pallas_call(body, out_shape=jax.ShapeDtypeStruct((2 * ROWS, HD), f32),...]
    dot_general x6 -> x0, matrix products: 48.6 us -> none  [the longest x1 13 us: score_pair(): jnp.einsum('qhe,khe->qhk', q_pair, key_pair, preferred_element_type=jnp.f...]
    all_gather x2 -> x0, local copies, waits for them, and re-layouts: 17.5 us -> none  [the longest x1 8.91 us: shards(): lax.all_gather(val_tan_flat, 'blk', axis=0, tiled=True)]
    reshape x2 -> x0, local copies, waits for them, and re-layouts: 17.3 us -> none  [the longest x1 8.68 us: shards(): all_keys.reshape(whole_count, HEADS, HEAD)]
    unnamed x18 -> x16, local copies, waits for them, and re-layouts: 2.95 us -> 7.58 us
  transfers between devices with their start and end apart: 5 -> 0, of which waited for: 5 -> 0; matrix products, arithmetic and copies ran while one was open for 24% -> 0% of each run, Pallas kernels for 0% -> 0%
where the time goes in v1:
time: 77.9 us; the launch traced here: 77.4 us
  Pallas kernels  66.7 us (86%)
  local copies, waits for them, and re-layouts  7.58 us (10%)
  other arithmetic  2.46 us (3%)
    pallas_call x1, Pallas kernels, attention(): pl.pallas_call(body, out_shape=jax.ShapeDtypeStruct((2 * ROWS, HD), f32),...  66.7 us
    unnamed x16, local copies, waits for them, and re-layouts  7.58 us

profile of v1, /device:TPU:1, one launch (start us, length us, event | category | flops | bytes accessed | tf_op | source)
XLA Modules:
  0.0 77.4 jit_solution(2109236971723290949)
XLA Ops:
  0.6 0.7 reduce
  1.3 0.7 reduce.1
  2.1 0.0 copy-start
  2.1 1.0 %copy-done = bf16[1,128,1536]{2,1,0:T(8,128)(2,1)S(1)} copy-done((bf16[1,128,1536]{2,1,0:T(8,128)(2,1)S(1)}, bf16[1,128,1536]{2,1,0:T(8,128)(2,1)}, u32[]{:S(2)}) %copy-start) | copy-done | bytes 393240
  3.1 0.0 copy-start.1
  3.1 1.0 %copy-done.1 = bf16[1,128,1536]{2,1,0:T(8,128)(2,1)S(1)} copy-done((bf16[1,128,1536]{2,1,0:T(8,128)(2,1)S(1)}, bf16[1,128,1536]{2,1,0:T(8,128)(2,1)}, u32[]{:S(2)}) %copy-start.1) | copy-done | bytes 393240
  4.1 0.0 copy-start.2
  4.1 1.0 %copy-done.2 = bf16[1,128,1536]{2,1,0:T(8,128)(2,1)S(1)} copy-done((bf16[1,128,1536]{2,1,0:T(8,128)(2,1)S(1)}, bf16[1,128,1536]{2,1,0:T(8,128)(2,1)}, u32[]{:S(2)}) %copy-start.2) | copy-done | bytes 393240
  5.1 0.0 copy-start.3
  5.1 1.0 %copy-done.3 = bf16[1,128,1536]{2,1,0:T(8,128)(2,1)S(1)} copy-done((bf16[1,128,1536]{2,1,0:T(8,128)(2,1)S(1)}, bf16[1,128,1536]{2,1,0:T(8,128)(2,1)}, u32[]{:S(2)}) %copy-start.3) | copy-done | bytes 393240
  6.1 0.0 copy-start.4
  6.1 1.0 %copy-done.4 = bf16[1,128,1536]{2,1,0:T(8,128)(2,1)S(1)} copy-done((bf16[1,128,1536]{2,1,0:T(8,128)(2,1)S(1)}, bf16[1,128,1536]{2,1,0:T(8,128)(2,1)}, u32[]{:S(2)}) %copy-start.4) | copy-done | bytes 393240
  7.0 0.0 copy-start.5
  7.1 1.0 %copy-done.5 = bf16[1,128,1536]{2,1,0:T(8,128)(2,1)S(1)} copy-done((bf16[1,128,1536]{2,1,0:T(8,128)(2,1)S(1)}, bf16[1,128,1536]{2,1,0:T(8,128)(2,1)}, u32[]{:S(2)}) %copy-start.5) | copy-done | bytes 393240
  8.0 0.0 copy-start.6
  8.0 1.0 %copy-done.6 = bf16[96,1536]{1,0:T(8,128)(2,1)S(1)} copy-done((bf16[96,1536]{1,0:T(8,128)(2,1)S(1)}, bf16[96,1536]{1,0:T(8,128)(2,1)}, u32[]{:S(2)}) %copy-start.6) | copy-done | bytes 294936
  9.0 0.0 copy-start.7
  9.0 0.7 copy-done.7
  9.7 66.7 %attention.1 = f32[256,1536]{1,0:T(8,128)S(1)} custom-call(bf16[1,128,1536]{2,1,0:T(8,128)(2,1)S(1)} %copy-done, bf16[1,128,1536]{2,1,0:T(8,128)(2,1)S(1)} %copy-done.1, bf16[1,128,1536]{2,1,0:T(8,128)(2,1)S(1)} %copy-done.2, bf16[1,128,1536]{2,1,0:T(8,128)(2,1)S(1)} %copy-done.3, bf16[1,128,1536]{2,1,0:T(8,128)(2,1)S(1)} %copy-done.4, ...), custom_call_target="tpu_custom_call" | custom-call | flops 7000000000 | bytes 10000000 | tf_op jit(solution)/shard_map/attention/pallas_call | solution.py:291
  76.4 1.0 %fusion.1 = (bf16[1,128,1536]{2,1,0:T(8,128)(2,1)}, bf16[1,128,1536]{2,1,0:T(8,128)(2,1)}) fusion(f32[256,1536]{1,0:T(8,128)S(1)} %attention.1, f32[1536]{0:T(1024)S(1)} %reduce.1, f32[1536]{0:T(1024)S(1)} %reduce), kind=kLoop, calls=%fused_computation.3 | loop fusion | flops 1179648 | bytes 2371584 | tf_op jit(solution)/shard_map/broadcast_in_dim | solution.py:329
Async XLA Ops:
  2.1 1.0 %copy-start = (bf16[1,128,1536]{2,1,0:T(8,128)(2,1)S(1)}, bf16[1,128,1536]{2,1,0:T(8,128)(2,1)}, u32[]{:S(2)}) copy-start(bf16[1,128,1536]{2,1,0:T(8,128)(2,1)} %q_hbm.1) | copy-start | bytes 1179652
  3.1 1.0 %copy-start.1 = (bf16[1,128,1536]{2,1,0:T(8,128)(2,1)S(1)}, bf16[1,128,1536]{2,1,0:T(8,128)(2,1)}, u32[]{:S(2)}) copy-start(bf16[1,128,1536]{2,1,0:T(8,128)(2,1)} %qt_hbm.1) | copy-start | bytes 1179652
  4.1 1.0 %copy-start.2 = (bf16[1,128,1536]{2,1,0:T(8,128)(2,1)S(1)}, bf16[1,128,1536]{2,1,0:T(8,128)(2,1)}, u32[]{:S(2)}) copy-start(bf16[1,128,1536]{2,1,0:T(8,128)(2,1)} %k_hbm.1) | copy-start | bytes 1179652
  5.1 1.0 %copy-start.3 = (bf16[1,128,1536]{2,1,0:T(8,128)(2,1)S(1)}, bf16[1,128,1536]{2,1,0:T(8,128)(2,1)}, u32[]{:S(2)}) copy-start(bf16[1,128,1536]{2,1,0:T(8,128)(2,1)} %kt_hbm.1) | copy-start | bytes 1179652
  6.1 1.0 %copy-start.4 = (bf16[1,128,1536]{2,1,0:T(8,128)(2,1)S(1)}, bf16[1,128,1536]{2,1,0:T(8,128)(2,1)}, u32[]{:S(2)}) copy-start(bf16[1,128,1536]{2,1,0:T(8,128)(2,1)} %v_hbm.1) | copy-start | bytes 1179652
  7.0 1.0 %copy-start.5 = (bf16[1,128,1536]{2,1,0:T(8,128)(2,1)S(1)}, bf16[1,128,1536]{2,1,0:T(8,128)(2,1)}, u32[]{:S(2)}) copy-start(bf16[1,128,1536]{2,1,0:T(8,128)(2,1)} %vt_hbm.1) | copy-start | bytes 1179652
  8.0 1.0 %copy-start.6 = (bf16[96,1536]{1,0:T(8,128)(2,1)S(1)}, bf16[96,1536]{1,0:T(8,128)(2,1)}, u32[]{:S(2)}) copy-start(bf16[96,1536]{1,0:T(8,128)(2,1)} %w_hbm.1) | copy-start | bytes 884740
  9.0 0.7 copy-start.7

commit v2 on v1

--- a/solution.py
+++ b/solution.py
@@ -14,13 +14,13 @@
 NX = 4
 PER = 3
 KEYS = 512
-CHUNK = 256
 DP_ROWS = 96
 HALF = 768
 MESH = pl.DeviceIdType.MESH
 NT = (((1,), (1,)), ((), ()))
 ORDER = (0, 1, 3, 2)
 AHEAD = 3
+W_LAG = 2
 
 epsilon = 1e-06
 
@@ -33,10 +33,10 @@
 
 
 def body(
-    q_hbm, qt_hbm, k_hbm, kt_hbm, v_hbm, vt_hbm, scale_ref, w_hbm, out_ref,
-    raw, kv, kv_send, qb, q_send, pv, uv, tot, mom, ret, att, w_mine, w_other,
+    q_hbm, qt_hbm, k_hbm, kt_hbm, v_hbm, vt_hbm, w_hbm, gate_hbm, gate_tan_hbm, scale_hbm, out_ref, tan_ref,
+    raw, gates, scale_ref, kv, kv_send, qb, q_send, pv, uv, tot, mom, ret, att, w_mine, w_other,
     load_sem, xs, xr, qs, qr, ys, yr, cs, cr, ds, dr, rs, rr,
-    w_load, os, orr, ps, pr, ms, mr, ws, wr,
+    g_load, s_load, w_load, os, orr, ps, pr, ms, mr, ws, wr,
 ):
     blk, dp = lax.axis_index("blk"), lax.axis_index("dp")
     y, x, c = blk // 8, (blk // 2) % NX, blk % 2
@@ -64,6 +64,12 @@
     my_cols = pl.ds(pl.multiple_of(c * HALF, HALF), HALF)
     w_copy = pltpu.make_async_copy(w_hbm.at[:, my_cols], w_mine.at[my_rows], w_load)
     w_copy.start()
+    for n, src in enumerate((gate_hbm, gate_tan_hbm)):
+        copy = pltpu.make_async_copy(src, gates.at[pl.ds(n, 1)], g_load.at[n])
+        copy.start()
+        loads.append(copy)
+    s_copy = pltpu.make_async_copy(scale_hbm, scale_ref, s_load)
+    s_copy.start()
     pl.semaphore_wait(barrier, len(peers))
 
     sent = []
@@ -125,55 +131,64 @@
                 dst, qb.at[i, pl.ds(j * ROWS, ROWS)], qs.at[i, j], qr.at[i, j], at_x(j)
             )
 
-    w_copy.wait()
-    outer_in = remote(w_mine.at[my_rows], w_mine.at[my_rows], os, orr, outer)
+    def piece(distance, other):
+        row = (((z + distance + 8) % 8) * 2 + (1 - yh if other else yh)) * DP_ROWS
+        return w_mine.at[pl.ds(pl.multiple_of(row, DP_ROWS), DP_ROWS)], w_other.at[
+            pl.ds(pl.multiple_of(row, DP_ROWS), DP_ROWS)
+        ]
+
+    up_in, down_in, w_in = {}, {}, []
+
+    def w_send(distance, other, going):
+        if going > 0:
+            n = 2 * distance + other
+            here = piece(-distance, other)[0]
+            up_in[n] = remote(here, here, ps.at[n], pr.at[n], z_up)
+        else:
+            n = 2 * distance + other if distance < 3 else 6
+            here = piece(distance, other)[0]
+            down_in[n] = remote(here, here, ms.at[n], mr.at[n], z_down)
+
+    def w_share(distance, other, n):
+        here, there = piece(distance, other)
+        w_in.append(remote(here, there, ws.at[n], wr.at[n], c_peer))
+
+    def w_pass(n):
+        up_in[n].wait_recv()
+        down_in[n].wait_recv()
+        distance, other = n // 2 + 1, n % 2
+        if n < 5:
+            w_send(distance, other, 1)
+        if n < 4:
+            w_send(distance, other, -1)
+        if n == 5:
+            w_send(3, 1, -1)
+        w_share(-distance, other, 2 + n)
+        w_share(distance, other if n < 6 else 1, 9 + n)
 
     for n in range(4):
         loads[n].wait()
     for j in ORDER:
         send_keys(0, j)
+    w_copy.wait()
+    outer_in = remote(w_mine.at[my_rows], w_mine.at[my_rows], os, orr, outer)
+    w_send(0, 0, 1)
+    w_send(0, 0, -1)
     loads[4].wait()
     loads[5].wait()
     for j in ORDER:
         send_queries(0, j)
 
-    def w_block(step):
-        block = (z + step + 8) % 8
-        return pl.ds(pl.multiple_of(block * 192, 192), 192)
-
-    w_in = []
-    up_in, down_in = {}, {}
-
-    def w_pass(step):
-        if step == 0:
-            outer_in.wait_recv()
-        else:
-            up_in[step].wait_recv()
-            if step <= 3:
-                down_in[step].wait_recv()
-        low = w_block(-step)
-        if step < 4:
-            up_in[step + 1] = remote(
-                w_mine.at[low], w_mine.at[low], ps.at[step], pr.at[step], z_up
-            )
-        w_in.append(remote(w_mine.at[low], w_other.at[low], ws.at[step], wr.at[step], c_peer))
-        if step <= 3:
-            high = w_block(step)
-            if step < 3:
-                down_in[step + 1] = remote(
-                    w_mine.at[high], w_mine.at[high], ms.at[step], mr.at[step], z_down
-                )
-            if step > 0:
-                w_in.append(
-                    remote(w_mine.at[high], w_other.at[high], ws.at[4 + step], wr.at[4 + step], c_peer)
-                )
-
-    w_pass(0)
     for i in range(1, PER):
         for j in ORDER:
             send_keys(i, j)
         for j in ORDER:
             send_queries(i, j)
+    outer_in.wait_recv()
+    w_send(0, 1, 1)
+    w_send(0, 1, -1)
+    w_share(0, 0, 0)
+    w_share(0, 1, 1)
 
     steps = [(i, j) for i in range(PER) for j in ORDER]
     passed = 0
@@ -191,41 +206,35 @@
         scale = scale_ref[PER * x + i] * (1.0 / math.sqrt(HEAD))
         rate = scale * math.log2(math.e)
 
-        def chunk(n, carry):
-            rows = pl.ds(pl.multiple_of(n * CHUNK, CHUNK), CHUNK)
-            queries = qb[i, rows, :]
-            scores = lax.dot_general(
-                queries[:, 128:256], kv[i, j, :, 0:128], NT, preferred_element_type=jnp.float32
-            )
-            slopes = lax.dot_general(
-                queries, kv[i, j, :, 0:256], NT, preferred_element_type=jnp.float32
-            )
-            probs = jnp.exp2(scores * rate)
-            weighted = probs * (slopes * scale)
-            p_sum = probs[:, 0:128]
-            w_sum = weighted[:, 0:128]
-            for part in range(1, KEYS // 128):
-                p_sum = p_sum + probs[:, part * 128 : (part + 1) * 128]
-                w_sum = w_sum + weighted[:, part * 128 : (part + 1) * 128]
-            p_mix = jnp.dot(
-                probs.astype(jnp.bfloat16), kv[i, j, :, 256:512], preferred_element_type=jnp.float32
-            )
-            w_mix = jnp.dot(
-                weighted.astype(jnp.bfloat16), kv[i, j, :, 256:384], preferred_element_type=jnp.float32
-            )
-            if j == 0:
-                tot[rows, :] = p_sum
-                mom[rows, :] = w_sum
-                pv[rows, :] = p_mix
-                uv[rows, :] = w_mix
-            else:
-                tot[rows, :] += p_sum
-                mom[rows, :] += w_sum
-                pv[rows, :] += p_mix
-                uv[rows, :] += w_mix
-            return carry
-
-        lax.fori_loop(0, KEYS // CHUNK, chunk, 0)
+        scores = lax.dot_general(
+            qb[i, :, 128:256], kv[i, j, :, 0:128], NT, preferred_element_type=jnp.float32
+        )
+        slopes = lax.dot_general(
+            qb[i], kv[i, j, :, 0:256], NT, preferred_element_type=jnp.float32
+        )
+        probs = jnp.exp2(scores * rate)
+        weighted = probs * (slopes * scale)
+        p_sum = probs[:, 0:128]
+        w_sum = weighted[:, 0:128]
+        for part in range(1, KEYS // 128):
+            p_sum = p_sum + probs[:, part * 128 : (part + 1) * 128]
+            w_sum = w_sum + weighted[:, part * 128 : (part + 1) * 128]
+        p_mix = jnp.dot(
+            probs.astype(jnp.bfloat16), kv[i, j, :, 256:512], preferred_element_type=jnp.float32
+        )
+        w_mix = jnp.dot(
+            weighted.astype(jnp.bfloat16), kv[i, j, :, 256:384], preferred_element_type=jnp.float32
+        )
+        if j == 0:
+            tot[...] = p_sum
+            mom[...] = w_sum
+            pv[...] = p_mix
+            uv[...] = w_mix
+        else:
+            tot[...] += p_sum
+            mom[...] += w_sum
+            pv[...] += p_mix
+            uv[...] += w_mix
 
     def finish(i):
         head = PER * x + i
@@ -247,13 +256,13 @@
                     ret.at[i, j - 1], att.at[:, cols], rs.at[i, j], rr.at[i, j], at_x(NX - j)
                 )
 
-    w_steps = {3: 1, 5: 2, 8: 3, 10: 4}
+    s_copy.wait()
     pass_up_to(AHEAD)
     relay(*steps[0])
     for n, (i, j) in enumerate(steps):
         pass_up_to(n + 1 + AHEAD)
-        if n in w_steps:
-            w_pass(w_steps[n])
+        if 0 <= n - W_LAG < 7:
+            w_pass(n - W_LAG)
         if n + 1 < len(steps):
             relay(*steps[n + 1])
         if j == 0:
@@ -265,6 +274,8 @@
         if j == ORDER[-1]:
             finish(i)
 
+    loads[6].wait()
+    loads[7].wait()
     for copy in w_in:
         copy.wait_recv()
     for copy in r_in.values():
@@ -273,10 +284,13 @@
     def project(n, carry):
         for half, offset in ((w_mine, c), (w_other, 1 - c)):
             cols = pl.ds(pl.multiple_of(offset * HALF + n * 256, 256), 256)
-            out_ref[:, cols] = jnp.dot(
+            projected = jnp.dot(
                 att[...], half[:, pl.ds(pl.multiple_of(n * 256, 256), 256)],
                 preferred_element_type=jnp.float32,
             )
+            gate, gate_tan = gates[0:1, cols], gates[1:2, cols]
+            out_ref[:, cols] = gate * projected[0:ROWS]
+            tan_ref[:, cols] = gate_tan * projected[0:ROWS] + gate * projected[ROWS:]
         return carry
 
     lax.fori_loop(0, HALF // 256, project, 0)
@@ -284,17 +298,19 @@
         copy.wait_send()
 
 
-def attention(q_raw, q_tan, k_raw, k_tan, values, values_tan, head_scale, w_out):
+def attention(q_raw, q_tan, k_raw, k_tan, values, values_tan, w_out, gate, gate_tan, head_scale):
     bf16, f32 = jnp.bfloat16, jnp.float32
     dma = pltpu.SemaphoreType.DMA
     any_spec = pl.BlockSpec(memory_space=pl.ANY)
     return pl.pallas_call(
         body,
-        out_shape=jax.ShapeDtypeStruct((2 * ROWS, HD), f32),
-        in_specs=[any_spec] * 6 + [pl.BlockSpec(memory_space=pltpu.SMEM), any_spec],
-        out_specs=pl.BlockSpec(memory_space=pltpu.VMEM),
+        out_shape=[jax.ShapeDtypeStruct((ROWS, HD), f32)] * 2,
+        in_specs=[any_spec] * 10,
+        out_specs=[pl.BlockSpec(memory_space=pltpu.VMEM)] * 2,
         scratch_shapes=[
             pltpu.VMEM((6, ROWS, HD), bf16),
+            pltpu.VMEM((2, HD), f32),
+            pltpu.SMEM((HEADS,), f32),
             pltpu.VMEM((PER, NX, KEYS, 512), bf16),
             pltpu.VMEM((PER, NX - 1, ROWS, 512), bf16),
             pltpu.VMEM((PER, KEYS, 256), bf16),
@@ -310,8 +326,8 @@
             dma((6,)),
         ]
         + [dma((PER, NX))] * 12
-        + [dma, dma, dma]
-        + [dma((4,)), dma((4,)), dma((3,)), dma((3,)), dma((8,)), dma((8,))],
+        + [dma((2,)), dma, dma, dma, dma]
+        + [dma((7,)), dma((7,)), dma((7,)), dma((7,)), dma((16,)), dma((16,))],
         compiler_params=pltpu.CompilerParams(
             collective_id=0, has_side_effects=True, vmem_limit_bytes=48 * 1024 * 1024
         ),
@@ -319,14 +335,15 @@
             flops=7_000_000_000, bytes_accessed=10_000_000, transcendentals=3_200_000
         ),
         name="attention",
-    )(q_raw, q_tan, k_raw, k_tan, values, values_tan, head_scale, w_out)
+    )(q_raw, q_tan, k_raw, k_tan, values, values_tan, w_out, gate, gate_tan, head_scale)
 
 
 def shards(q_raw, q_tan, k_raw, k_tan, values, values_tan, head_scale, w_out, gate, gate_tan):
-    projected = attention(q_raw, q_tan, k_raw, k_tan, values, values_tan, head_scale, w_out)
-    layer_out = (gate * projected[:ROWS]).astype(jnp.bfloat16)
-    layer_tan = (gate_tan * projected[:ROWS] + gate * projected[ROWS:]).astype(jnp.bfloat16)
-    return (layer_out[None], layer_tan[None])
+    arrays = (q_raw, q_tan, k_raw, k_tan, values, values_tan, w_out, gate, gate_tan, head_scale)
+    main, tangent = attention(
+        *(pltpu.with_memory_space_constraint(array, pltpu.HBM) for array in arrays)
+    )
+    return (main.astype(jnp.bfloat16)[None], tangent.astype(jnp.bfloat16)[None])
 
 
 def solution(mesh):

time: 77.9 us -> 59 us (0.76)
  Pallas kernels: 66.7 us -> 57.3 us
  local copies, waits for them, and re-layouts: 7.58 us -> 0 us
  other arithmetic: 2.46 us -> 0.96 us
    pallas_call x1, Pallas kernels: 66.7 us -> 57.3 us  [attention(): pl.pallas_call(body, out_shape=[jax.ShapeDtypeStruct((ROWS, HD), f32)] *...]
    unnamed x16 -> x0, local copies, waits for them, and re-layouts: 7.58 us -> none
    unnamed x2 -> x0, other arithmetic: 1.43 us -> none
where the time goes in v2:
time: 59 us; the launch traced here: 58.9 us
  Pallas kernels  57.3 us (97%)
  other arithmetic  0.96 us (2%)
  between operations  0.64 us (1%)
    pallas_call x1, Pallas kernels, attention(): pl.pallas_call(body, out_shape=[jax.ShapeDtypeStruct((ROWS, HD), f32)] *...  57.3 us

profile of v2, /device:TPU:1, one launch (start us, length us, event | category | flops | bytes accessed | tf_op | source)
XLA Modules:
  0.0 58.9 jit_solution(18165201339532522361)
XLA Ops:
  0.6 57.3 %attention.1 = (f32[128,1536]{1,0:T(8,128)S(1)}, f32[128,1536]{1,0:T(8,128)S(1)}) custom-call(bf16[1,128,1536]{2,1,0:T(8,128)(2,1)} %q_hbm.1, bf16[1,128,1536]{2,1,0:T(8,128)(2,1)} %qt_hbm.1, bf16[1,128,1536]{2,1,0:T(8,128)(2,1)} %k_hbm.1, bf16[1,128,1536]{2,1,0:T(8,128)(2,1)} %kt_hbm.1, bf16[1,128,1536]{2,1,0:T(8,128)(2,1)} %v_hbm.1, ...), custom_call_target="tpu_custom_call" | custom-call | flops 7000000000 | bytes 10000000 | tf_op jit(solution)/shard_map/attention/pallas_call | solution.py:305
  57.9 1.0 %convert_bitcast_fusion = (bf16[1,128,1536]{2,1,0:T(8,128)(2,1)}, bf16[1,128,1536]{2,1,0:T(8,128)(2,1)}) fusion(f32[128,1536]{1,0:T(8,128)S(1)} %get-tuple-element.5, f32[128,1536]{1,0:T(8,128)S(1)} %get-tuple-element.4), kind=kLoop, calls=%fused_computation | loop fusion | flops 393216 | bytes 2359296 | tf_op jit(solution)/shard_map/broadcast_in_dim | solution.py:346

commit v3 on v2

--- a/solution.py
+++ b/solution.py
@@ -20,7 +20,8 @@
 NT = (((1,), (1,)), ((), ()))
 ORDER = (0, 1, 3, 2)
 AHEAD = 3
-W_LAG = 2
+W_OTHER = 0
+W_PLAN = {1: (0,), 3: (1,), 5: (2,), 6: (3,), 7: (4,), 9: (5,), 10: (6,)}
 
 epsilon = 1e-06
 
@@ -34,9 +35,9 @@
 
 def body(
     q_hbm, qt_hbm, k_hbm, kt_hbm, v_hbm, vt_hbm, w_hbm, gate_hbm, gate_tan_hbm, scale_hbm, out_ref, tan_ref,
-    raw, gates, scale_ref, kv, kv_send, qb, q_send, pv, uv, tot, mom, ret, att, w_mine, w_other,
+    raw, gates, scale_ref, kv, kv_send, qb, q_send, pv, uv, tot, mom, ret, att, part, w_mine, w_other,
     load_sem, xs, xr, qs, qr, ys, yr, cs, cr, ds, dr, rs, rr,
-    g_load, s_load, w_load, os, orr, ps, pr, ms, mr, ws, wr,
+    go_clip, go_w, g_load, s_load, w_load, os, orr, ps, pr, ms, mr, ws, wr,
 ):
     blk, dp = lax.axis_index("blk"), lax.axis_index("dp")
     y, x, c = blk // 8, (blk // 2) % NX, blk % 2
@@ -52,9 +53,17 @@
     z_down = {"dp": ((z + 7) % 8) * 2 + yh, "blk": blk}
 
     barrier = pltpu.get_barrier_semaphore()
-    peers = [at_x(1), at_x(2), at_x(3), y_peer, c_peer, outer, z_up, z_down]
-    for peer in peers:
+
+    def greet(peer):
         pl.semaphore_signal(barrier, inc=1, device_id=peer, device_id_type=MESH)
+
+    for j in range(1, NX):
+        greet({"dp": dp, "blk": y * 8 + ((x + j) % NX) * 2})
+    greet({"dp": dp, "blk": (1 - y) * 8 + x * 2})
+    pl.when(c == 1)(lambda: greet({"dp": dp, "blk": y * 8 + x * 2}))
+    greet({"dp": z * 2 + (1 - yh), "blk": (1 - y) * 8 + x * 2 + 1})
+    greet({"dp": ((z + 1) % 8) * 2 + yh, "blk": y * 8 + x * 2 + 1})
+    greet({"dp": ((z + 7) % 8) * 2 + yh, "blk": y * 8 + x * 2 + 1})
     loads = []
     for n, src in enumerate((k_hbm, kt_hbm, v_hbm, vt_hbm, q_hbm, qt_hbm)):
         copy = pltpu.make_async_copy(src.at[0], raw.at[n], load_sem.at[n])
@@ -70,7 +79,16 @@
         loads.append(copy)
     s_copy = pltpu.make_async_copy(scale_hbm, scale_ref, s_load)
     s_copy.start()
-    pl.semaphore_wait(barrier, len(peers))
+
+    @pl.when(c == 0)
+    def _():
+        pl.semaphore_wait(barrier, 9)
+        pl.semaphore_signal(go_clip, inc=1, device_id=c_peer, device_id_type=MESH)
+
+    @pl.when(c == 1)
+    def _():
+        pl.semaphore_wait(go_clip, 1)
+
 
     sent = []
 
@@ -170,10 +188,6 @@
         loads[n].wait()
     for j in ORDER:
         send_keys(0, j)
-    w_copy.wait()
-    outer_in = remote(w_mine.at[my_rows], w_mine.at[my_rows], os, orr, outer)
-    w_send(0, 0, 1)
-    w_send(0, 0, -1)
     loads[4].wait()
     loads[5].wait()
     for j in ORDER:
@@ -184,11 +198,20 @@
             send_keys(i, j)
         for j in ORDER:
             send_queries(i, j)
-    outer_in.wait_recv()
-    w_send(0, 1, 1)
-    w_send(0, 1, -1)
+    @pl.when(c == 1)
+    def _():
+        pl.semaphore_wait(barrier, 6)
+        pl.semaphore_signal(go_w, inc=1, device_id=c_peer, device_id_type=MESH)
+
+    @pl.when(c == 0)
+    def _():
+        pl.semaphore_wait(go_w, 1)
+
+    w_copy.wait()
+    outer_in = remote(w_mine.at[my_rows], w_mine.at[my_rows], os, orr, outer)
+    w_send(0, 0, 1)
+    w_send(0, 0, -1)
     w_share(0, 0, 0)
-    w_share(0, 1, 1)
 
     steps = [(i, j) for i in range(PER) for j in ORDER]
     passed = 0
@@ -237,8 +260,8 @@
             uv[...] += w_mix
 
     def finish(i):
-        head = PER * x + i
-        cols = pl.ds(pl.multiple_of(head * HEAD, HEAD), HEAD)
+        first = x * 256 + i * HEAD if i < 2 else 1024 + x * HEAD
+        cols = pl.ds(pl.multiple_of(first, HEAD), HEAD)
         for j in (2, 1, 3, 0):
             rows = pl.ds(j * ROWS, ROWS)
             inv = 1.0 / jnp.sum(tot[rows, :], -1, keepdims=True)
@@ -261,8 +284,13 @@
     relay(*steps[0])
     for n, (i, j) in enumerate(steps):
         pass_up_to(n + 1 + AHEAD)
-        if 0 <= n - W_LAG < 7:
-            w_pass(n - W_LAG)
+        if n == W_OTHER:
+            outer_in.wait_recv()
+            w_send(0, 1, 1)
+            w_send(0, 1, -1)
+            w_share(0, 1, 1)
+        for arrival in W_PLAN.get(n, ()):
+            w_pass(arrival)
         if n + 1 < len(steps):
             relay(*steps[n + 1])
         if j == 0:
@@ -276,24 +304,33 @@
 
     loads[6].wait()
     loads[7].wait()
+
+    def product(half, col, first, depth):
+        cols = pl.ds(col, 256)
+        rows = [half[pl.ds(k * 384 + first, depth), cols] for k in range(NX)]
+        start = 0 if first == 0 else 1024
+        return jnp.dot(
+            att[:, start : start + NX * depth], jnp.concatenate(rows, 0),
+            preferred_element_type=jnp.float32,
+        )
+
     for copy in w_in:
         copy.wait_recv()
-    for copy in r_in.values():
-        copy.wait_recv()
-
-    def project(n, carry):
-        for half, offset in ((w_mine, c), (w_other, 1 - c)):
-            cols = pl.ds(pl.multiple_of(offset * HALF + n * 256, 256), 256)
-            projected = jnp.dot(
-                att[...], half[:, pl.ds(pl.multiple_of(n * 256, 256), 256)],
-                preferred_element_type=jnp.float32,
-            )
+    for i in range(PER - 1):
+        for j in ORDER[1:]:
+            r_in[i, j].wait_recv()
+    for n, half in enumerate((w_mine, w_other)):
+        for col in range(0, HALF, 256):
+            part[n, :, col : col + 256] = product(half, col, 0, 256)
+    for j in ORDER[1:]:
+        r_in[PER - 1, j].wait_recv()
+    for n, (half, offset) in enumerate(((w_mine, c), (w_other, 1 - c))):
+        for col in range(0, HALF, 256):
+            projected = part[n, :, col : col + 256] + product(half, col, 256, HEAD)
+            cols = pl.ds(pl.multiple_of(offset * HALF + col, 256), 256)
             gate, gate_tan = gates[0:1, cols], gates[1:2, cols]
             out_ref[:, cols] = gate * projected[0:ROWS]
             tan_ref[:, cols] = gate_tan * projected[0:ROWS] + gate * projected[ROWS:]
-        return carry
-
-    lax.fori_loop(0, HALF // 256, project, 0)
     for copy in sent:
         copy.wait_send()
 
@@ -321,11 +358,13 @@
             pltpu.VMEM((KEYS, 128), f32),
             pltpu.VMEM((PER, NX - 1, 2 * ROWS, HEAD), bf16),
             pltpu.VMEM((2 * ROWS, HD), bf16),
+            pltpu.VMEM((2, 2 * ROWS, HALF), f32),
             pltpu.VMEM((HD, HALF), bf16),
             pltpu.VMEM((HD, HALF), bf16),
             dma((6,)),
         ]
         + [dma((PER, NX))] * 12
+        + [pltpu.SemaphoreType.REGULAR] * 2
         + [dma((2,)), dma, dma, dma, dma]
         + [dma((7,)), dma((7,)), dma((7,)), dma((7,)), dma((16,)), dma((16,))],
         compiler_params=pltpu.CompilerParams(

time: 59 us -> 55.2 us (0.936)
  Pallas kernels: 57.3 us -> 53.5 us
    pallas_call x1, Pallas kernels: 57.3 us -> 53.5 us  [attention(): pl.pallas_call(body, out_shape=[jax.ShapeDtypeStruct((ROWS, HD), f32)] *...]
where the time goes in v3:
time: 55.2 us; the launch traced here: 55.1 us
  Pallas kernels  53.5 us (97%)
  other arithmetic  0.96 us (2%)
  between operations  0.64 us (1%)
    pallas_call x1, Pallas kernels, attention(): pl.pallas_call(body, out_shape=[jax.ShapeDtypeStruct((ROWS, HD), f32)] *...  53.5 us

profile of v3, /device:TPU:1, one launch (start us, length us, event | category | flops | bytes accessed | tf_op | source)
XLA Modules:
  0.0 55.1 jit_solution(4558342539667028004)
XLA Ops:
  0.6 53.5 %attention.1 = (f32[128,1536]{1,0:T(8,128)S(1)}, f32[128,1536]{1,0:T(8,128)S(1)}) custom-call(bf16[1,128,1536]{2,1,0:T(8,128)(2,1)} %q_hbm.1, bf16[1,128,1536]{2,1,0:T(8,128)(2,1)} %qt_hbm.1, bf16[1,128,1536]{2,1,0:T(8,128)(2,1)} %k_hbm.1, bf16[1,128,1536]{2,1,0:T(8,128)(2,1)} %kt_hbm.1, bf16[1,128,1536]{2,1,0:T(8,128)(2,1)} %v_hbm.1, ...), custom_call_target="tpu_custom_call" | custom-call | flops 7000000000 | bytes 10000000 | tf_op jit(solution)/shard_map/attention/pallas_call | solution.py:342
  54.1 1.0 %convert_bitcast_fusion = (bf16[1,128,1536]{2,1,0:T(8,128)(2,1)}, bf16[1,128,1536]{2,1,0:T(8,128)(2,1)}) fusion(f32[128,1536]{1,0:T(8,128)S(1)} %get-tuple-element.5, f32[128,1536]{1,0:T(8,128)S(1)} %get-tuple-element.4), kind=kLoop, calls=%fused_computation | loop fusion | flops 393216 | bytes 2359296 | tf_op jit(solution)/shard_map/broadcast_in_dim | solution.py:385

commit v4 on v3

--- a/solution.py
+++ b/solution.py
@@ -19,9 +19,8 @@
 MESH = pl.DeviceIdType.MESH
 NT = (((1,), (1,)), ((), ()))
 ORDER = (0, 1, 3, 2)
-AHEAD = 3
-W_OTHER = 0
-W_PLAN = {1: (0,), 3: (1,), 5: (2,), 6: (3,), 7: (4,), 9: (5,), 10: (6,)}
+AHEAD = 5
+W_PLAN = {0: (0,), 1: (1,), 3: (2,), 5: (3,), 7: (4,), 9: (5,), 11: (6,)}
 
 epsilon = 1e-06
 
@@ -194,10 +193,8 @@
         send_queries(0, j)
 
     for i in range(1, PER):
-        for j in ORDER:
-            send_keys(i, j)
-        for j in ORDER:
-            send_queries(i, j)
+        send_keys(i, 0)
+
     @pl.when(c == 1)
     def _():
         pl.semaphore_wait(barrier, 6)
@@ -212,6 +209,11 @@
     w_send(0, 0, 1)
     w_send(0, 0, -1)
     w_share(0, 0, 0)
+    for i in range(1, PER):
+        for j in ORDER[1:]:
+            send_keys(i, j)
+        for j in ORDER:
+            send_queries(i, j)
 
     steps = [(i, j) for i in range(PER) for j in ORDER]
     passed = 0
@@ -260,8 +262,6 @@
             uv[...] += w_mix
 
     def finish(i):
-        first = x * 256 + i * HEAD if i < 2 else 1024 + x * HEAD
-        cols = pl.ds(pl.multiple_of(first, HEAD), HEAD)
         for j in (2, 1, 3, 0):
             rows = pl.ds(j * ROWS, ROWS)
             inv = 1.0 / jnp.sum(tot[rows, :], -1, keepdims=True)
@@ -270,25 +270,24 @@
             main = (mixed * inv).astype(jnp.bfloat16)
             tangent = ((uv[rows, :] + pv[rows, 128:256] - mixed * moment) * inv).astype(jnp.bfloat16)
             if j == 0:
-                att[0:ROWS, cols] = main
-                att[ROWS : 2 * ROWS, cols] = tangent
+                att[i, x, 0:ROWS, :] = main
+                att[i, x, ROWS : 2 * ROWS, :] = tangent
             else:
                 ret[i, j - 1, 0:ROWS, :] = main
                 ret[i, j - 1, ROWS : 2 * ROWS, :] = tangent
                 r_in[i, j] = remote(
-                    ret.at[i, j - 1], att.at[:, cols], rs.at[i, j], rr.at[i, j], at_x(NX - j)
+                    ret.at[i, j - 1], att.at[i, x], rs.at[i, j], rr.at[i, j], at_x(NX - j)
                 )
 
     s_copy.wait()
+    outer_in.wait_recv()
+    w_send(0, 1, 1)
+    w_send(0, 1, -1)
+    w_share(0, 1, 1)
     pass_up_to(AHEAD)
     relay(*steps[0])
     for n, (i, j) in enumerate(steps):
         pass_up_to(n + 1 + AHEAD)
-        if n == W_OTHER:
-            outer_in.wait_recv()
-            w_send(0, 1, 1)
-            w_send(0, 1, -1)
-            w_share(0, 1, 1)
         for arrival in W_PLAN.get(n, ()):
             w_pass(arrival)
         if n + 1 < len(steps):
@@ -305,12 +304,11 @@
     loads[6].wait()
     loads[7].wait()
 
-    def product(half, col, first, depth):
-        cols = pl.ds(col, 256)
-        rows = [half[pl.ds(k * 384 + first, depth), cols] for k in range(NX)]
-        start = 0 if first == 0 else 1024
+    def product(half, col, heads):
+        pairs = [(i, k) for k in range(NX) for i in heads]
+        rows = [half[pl.ds((PER * k + i) * HEAD, HEAD), pl.ds(col, 256)] for i, k in pairs]
         return jnp.dot(
-            att[:, start : start + NX * depth], jnp.concatenate(rows, 0),
+            jnp.concatenate([att[i, k] for i, k in pairs], 1), jnp.concatenate(rows, 0),
             preferred_element_type=jnp.float32,
         )
 
@@ -321,12 +319,12 @@
             r_in[i, j].wait_recv()
     for n, half in enumerate((w_mine, w_other)):
         for col in range(0, HALF, 256):
-            part[n, :, col : col + 256] = product(half, col, 0, 256)
+            part[n, :, col : col + 256] = product(half, col, (0, 1))
     for j in ORDER[1:]:
         r_in[PER - 1, j].wait_recv()
     for n, (half, offset) in enumerate(((w_mine, c), (w_other, 1 - c))):
         for col in range(0, HALF, 256):
-            projected = part[n, :, col : col + 256] + product(half, col, 256, HEAD)
+            projected = part[n, :, col : col + 256] + product(half, col, (2,))
             cols = pl.ds(pl.multiple_of(offset * HALF + col, 256), 256)
             gate, gate_tan = gates[0:1, cols], gates[1:2, cols]
             out_ref[:, cols] = gate * projected[0:ROWS]
@@ -357,7 +355,7 @@
             pltpu.VMEM((KEYS, 128), f32),
             pltpu.VMEM((KEYS, 128), f32),
             pltpu.VMEM((PER, NX - 1, 2 * ROWS, HEAD), bf16),
-            pltpu.VMEM((2 * ROWS, HD), bf16),
+            pltpu.VMEM((PER, NX, 2 * ROWS, HEAD), bf16),
             pltpu.VMEM((2, 2 * ROWS, HALF), f32),
             pltpu.VMEM((HD, HALF), bf16),
             pltpu.VMEM((HD, HALF), bf16),

time: 55.2 us -> 52.5 us (0.951)
  Pallas kernels: 53.5 us -> 50.7 us
    pallas_call x1, Pallas kernels: 53.5 us -> 50.7 us  [attention(): pl.pallas_call(body, out_shape=[jax.ShapeDtypeStruct((ROWS, HD), f32)] *...]
where the time goes in v4:
time: 52.5 us; the launch traced here: 52.3 us
  Pallas kernels  50.7 us (97%)
  other arithmetic  0.96 us (2%)
  between operations  0.64 us (1%)
    pallas_call x1, Pallas kernels, attention(): pl.pallas_call(body, out_shape=[jax.ShapeDtypeStruct((ROWS, HD), f32)] *...  50.7 us

profile of v4, /device:TPU:1, one launch (start us, length us, event | category | flops | bytes accessed | tf_op | source)
XLA Modules:
  0.0 52.3 jit_solution(30301529341613522)
XLA Ops:
  0.6 50.7 %attention.1 = (f32[128,1536]{1,0:T(8,128)S(1)}, f32[128,1536]{1,0:T(8,128)S(1)}) custom-call(bf16[1,128,1536]{2,1,0:T(8,128)(2,1)} %q_hbm.1, bf16[1,128,1536]{2,1,0:T(8,128)(2,1)} %qt_hbm.1, bf16[1,128,1536]{2,1,0:T(8,128)(2,1)} %k_hbm.1, bf16[1,128,1536]{2,1,0:T(8,128)(2,1)} %kt_hbm.1, bf16[1,128,1536]{2,1,0:T(8,128)(2,1)} %v_hbm.1, ...), custom_call_target="tpu_custom_call" | custom-call | flops 7000000000 | bytes 10000000 | tf_op jit(solution)/shard_map/attention/pallas_call | solution.py:340
  51.4 1.0 %convert_bitcast_fusion = (bf16[1,128,1536]{2,1,0:T(8,128)(2,1)}, bf16[1,128,1536]{2,1,0:T(8,128)(2,1)}) fusion(f32[128,1536]{1,0:T(8,128)S(1)} %get-tuple-element.5, f32[128,1536]{1,0:T(8,128)S(1)} %get-tuple-element.4), kind=kLoop, calls=%fused_computation | loop fusion | flops 393216 | bytes 2359296 | tf_op jit(solution)/shard_map/broadcast_in_dim | solution.py:383

commit v5 on v4

--- a/solution.py
+++ b/solution.py
@@ -20,6 +20,8 @@
 NT = (((1,), (1,)), ((), ()))
 ORDER = (0, 1, 3, 2)
 AHEAD = 5
+OWN, MATE, ACROSS, DIAGONAL = range(4)
+SPLIT = 96
 W_PLAN = {0: (0,), 1: (1,), 3: (2,), 5: (3,), 7: (4,), 9: (5,), 11: (6,)}
 
 epsilon = 1e-06
@@ -36,7 +38,7 @@
     q_hbm, qt_hbm, k_hbm, kt_hbm, v_hbm, vt_hbm, w_hbm, gate_hbm, gate_tan_hbm, scale_hbm, out_ref, tan_ref,
     raw, gates, scale_ref, kv, kv_send, qb, q_send, pv, uv, tot, mom, ret, att, part, w_mine, w_other,
     load_sem, xs, xr, qs, qr, ys, yr, cs, cr, ds, dr, rs, rr,
-    go_clip, go_w, g_load, s_load, w_load, os, orr, ps, pr, ms, mr, ws, wr,
+    fs, fr, go_clip, go_w, g_load, s_load, w_load, os, orr, ps, pr, ms, mr, ws, wr,
 ):
     blk, dp = lax.axis_index("blk"), lax.axis_index("dp")
     y, x, c = blk // 8, (blk // 2) % NX, blk % 2
@@ -47,6 +49,7 @@
 
     y_peer = {"dp": dp, "blk": (1 - y) * 8 + x * 2 + c}
     c_peer = {"dp": dp, "blk": y * 8 + x * 2 + (1 - c)}
+    diagonal = {"dp": dp, "blk": (1 - y) * 8 + x * 2 + (1 - c)}
     outer = {"dp": z * 2 + (1 - yh), "blk": (1 - y) * 8 + x * 2 + c}
     z_up = {"dp": ((z + 1) % 8) * 2 + yh, "blk": blk}
     z_down = {"dp": ((z + 7) % 8) * 2 + yh, "blk": blk}
@@ -102,15 +105,34 @@
 
     x_in, q_in, y_in, c_in, d_in, r_in = {}, {}, {}, {}, {}, {}
 
+    last = (PER - 1, ORDER[-1])
+    tails = []
+
+    def keys_from(i, j, place, start=0, size=ROWS):
+        return kv.at[i, j, pl.ds(place * ROWS + start, size)]
+
     def forward(i, j):
-        own = kv.at[i, j, pl.ds(0, ROWS)]
-        y_in[i, j] = remote(own, kv.at[i, j, pl.ds(ROWS, ROWS)], ys.at[i, j], yr.at[i, j], y_peer)
-        c_in[i, j] = remote(own, kv.at[i, j, pl.ds(2 * ROWS, ROWS)], cs.at[i, j], cr.at[i, j], c_peer)
+        own = keys_from(i, j, OWN)
+        size = ROWS if (i, j) != last else SPLIT
+        y_in[i, j] = remote(
+            keys_from(i, j, OWN, 0, size), keys_from(i, j, ACROSS, 0, size),
+            ys.at[i, j], yr.at[i, j], y_peer,
+        )
+        if (i, j) == last:
+            for n, (place, peer) in enumerate(((ACROSS, y_peer), (DIAGONAL, diagonal))):
+                tails.append(
+                    remote(
+                        keys_from(i, j, OWN, SPLIT, ROWS - SPLIT),
+                        keys_from(i, j, place, SPLIT, ROWS - SPLIT), fs.at[n], fr.at[n], peer,
+                    )
+                )
+        c_in[i, j] = remote(own, keys_from(i, j, MATE), cs.at[i, j], cr.at[i, j], c_peer)
 
     def relay(i, j):
+        size = ROWS if (i, j) != last else SPLIT
         y_in[i, j].wait_recv()
         d_in[i, j] = remote(
-            kv.at[i, j, pl.ds(ROWS, ROWS)], kv.at[i, j, pl.ds(3 * ROWS, ROWS)],
+            keys_from(i, j, ACROSS, 0, size), keys_from(i, j, DIAGONAL, 0, size),
             ds.at[i, j], dr.at[i, j], c_peer,
         )
 
@@ -227,42 +249,43 @@
                 forward(i, j)
             passed += 1
 
-    def attend(i, j):
+    def attend(i, j, first, count, start=0, size=KEYS):
+        keys, rows = pl.ds(first, count), pl.ds(start, size)
         scale = scale_ref[PER * x + i] * (1.0 / math.sqrt(HEAD))
         rate = scale * math.log2(math.e)
 
         scores = lax.dot_general(
-            qb[i, :, 128:256], kv[i, j, :, 0:128], NT, preferred_element_type=jnp.float32
+            qb[i, rows, 128:256], kv[i, j, keys, 0:128], NT, preferred_element_type=jnp.float32
         )
         slopes = lax.dot_general(
-            qb[i], kv[i, j, :, 0:256], NT, preferred_element_type=jnp.float32
+            qb[i, rows, :], kv[i, j, keys, 0:256], NT, preferred_element_type=jnp.float32
         )
         probs = jnp.exp2(scores * rate)
         weighted = probs * (slopes * scale)
         p_sum = probs[:, 0:128]
         w_sum = weighted[:, 0:128]
-        for part in range(1, KEYS // 128):
+        for part in range(1, count // 128):
             p_sum = p_sum + probs[:, part * 128 : (part + 1) * 128]
             w_sum = w_sum + weighted[:, part * 128 : (part + 1) * 128]
         p_mix = jnp.dot(
-            probs.astype(jnp.bfloat16), kv[i, j, :, 256:512], preferred_element_type=jnp.float32
+            probs.astype(jnp.bfloat16), kv[i, j, keys, 256:512], preferred_element_type=jnp.float32
         )
         w_mix = jnp.dot(
-            weighted.astype(jnp.bfloat16), kv[i, j, :, 256:384], preferred_element_type=jnp.float32
+            weighted.astype(jnp.bfloat16), kv[i, j, keys, 256:384], preferred_element_type=jnp.float32
         )
         if j == 0:
-            tot[...] = p_sum
-            mom[...] = w_sum
-            pv[...] = p_mix
-            uv[...] = w_mix
+            tot[rows, :] = p_sum
+            mom[rows, :] = w_sum
+            pv[rows, :] = p_mix
+            uv[rows, :] = w_mix
         else:
-            tot[...] += p_sum
-            mom[...] += w_sum
-            pv[...] += p_mix
-            uv[...] += w_mix
-
-    def finish(i):
-        for j in (2, 1, 3, 0):
+            tot[rows, :] += p_sum
+            mom[rows, :] += w_sum
+            pv[rows, :] += p_mix
+            uv[rows, :] += w_mix
+
+    def finish(i, parts=(2, 1, 3, 0)):
+        for j in parts:
             rows = pl.ds(j * ROWS, ROWS)
             inv = 1.0 / jnp.sum(tot[rows, :], -1, keepdims=True)
             moment = jnp.sum(mom[rows, :], -1, keepdims=True) * inv
@@ -296,9 +319,18 @@
             for other in ORDER[1:]:
                 q_in[i, other].wait_recv()
         c_in[i, j].wait_recv()
-        d_in[i, j].wait_recv()
-        attend(i, j)
-        if j == ORDER[-1]:
+        if (i, j) == last:
+            attend(i, j, 0, KEYS // 2)
+            d_in[i, j].wait_recv()
+            for copy in tails:
+                copy.wait_recv()
+            for parts in ((2, 3), (1, 0)):
+                attend(i, j, KEYS // 2, KEYS // 2, min(parts) * ROWS, KEYS // 2)
+                finish(i, parts)
+        else:
+            d_in[i, j].wait_recv()
+            attend(i, j, 0, KEYS)
+        if j == ORDER[-1] and i < PER - 1:
             finish(i)
 
     loads[6].wait()
@@ -362,6 +394,7 @@
             dma((6,)),
         ]
         + [dma((PER, NX))] * 12
+        + [dma((2,)), dma((2,))]
         + [pltpu.SemaphoreType.REGULAR] * 2
         + [dma((2,)), dma, dma, dma, dma]
         + [dma((7,)), dma((7,)), dma((7,)), dma((7,)), dma((16,)), dma((16,))],

time: 52.5 us -> 51.7 us (0.985)
  Pallas kernels: 50.7 us -> 49.6 us
    pallas_call x1, Pallas kernels: 50.7 us -> 49.6 us  [attention(): pl.pallas_call(body, out_shape=[jax.ShapeDtypeStruct((ROWS, HD), f32)] *...]
where the time goes in v5:
time: 51.7 us; the launch traced here: 51.2 us
  Pallas kernels  49.6 us (96%)
  other arithmetic  0.96 us (2%)
  between operations  0.64 us (1%)
    pallas_call x1, Pallas kernels, attention(): pl.pallas_call(body, out_shape=[jax.ShapeDtypeStruct((ROWS, HD), f32)] *...  49.6 us

profile of v5, /device:TPU:1, one launch (start us, length us, event | category | flops | bytes accessed | tf_op | source)
XLA Modules:
  0.0 51.2 jit_solution(10340854338461331145)
XLA Ops:
  0.6 49.6 %attention.1 = (f32[128,1536]{1,0:T(8,128)S(1)}, f32[128,1536]{1,0:T(8,128)S(1)}) custom-call(bf16[1,128,1536]{2,1,0:T(8,128)(2,1)} %q_hbm.1, bf16[1,128,1536]{2,1,0:T(8,128)(2,1)} %qt_hbm.1, bf16[1,128,1536]{2,1,0:T(8,128)(2,1)} %k_hbm.1, bf16[1,128,1536]{2,1,0:T(8,128)(2,1)} %kt_hbm.1, bf16[1,128,1536]{2,1,0:T(8,128)(2,1)} %v_hbm.1, ...), custom_call_target="tpu_custom_call" | custom-call | flops 7000000000 | bytes 10000000 | tf_op jit(solution)/shard_map/attention/pallas_call | solution.py:372
  50.2 1.0 %convert_bitcast_fusion = (bf16[1,128,1536]{2,1,0:T(8,128)(2,1)}, bf16[1,128,1536]{2,1,0:T(8,128)(2,1)}) fusion(f32[128,1536]{1,0:T(8,128)S(1)} %get-tuple-element.5, f32[128,1536]{1,0:T(8,128)S(1)} %get-tuple-element.4), kind=kLoop, calls=%fused_computation | loop fusion | flops 393216 | bytes 2359296 | tf_op jit(solution)/shard_map/broadcast_in_dim | solution.py:416

commit v6 on v5

--- a/solution.py
+++ b/solution.py
@@ -22,7 +22,7 @@
 AHEAD = 5
 OWN, MATE, ACROSS, DIAGONAL = range(4)
 SPLIT = 96
-W_PLAN = {0: (0,), 1: (1,), 3: (2,), 5: (3,), 7: (4,), 9: (5,), 11: (6,)}
+W_PLAN = {0: (0,), 1: (1,), 3: (2,), 5: (3,), 7: (4,), 9: (5,)}
 
 epsilon = 1e-06
 
@@ -333,6 +333,7 @@
         if j == ORDER[-1] and i < PER - 1:
             finish(i)
 
+    w_pass(6)
     loads[6].wait()
     loads[7].wait()
 

time: 51.7 us -> 52.1 us (level)
  Pallas kernels: 49.6 us -> 50.4 us
    pallas_call x1, Pallas kernels: 49.6 us -> 50.4 us  [attention(): pl.pallas_call(body, out_shape=[jax.ShapeDtypeStruct((ROWS, HD), f32)] *...]
where the time goes in v6:
time: 52.1 us; the launch traced here: 52 us
  Pallas kernels  50.4 us (97%)
  other arithmetic  0.96 us (2%)
  between operations  0.64 us (1%)
    pallas_call x1, Pallas kernels, attention(): pl.pallas_call(body, out_shape=[jax.ShapeDtypeStruct((ROWS, HD), f32)] *...  50.4 us

profile of v6, /device:TPU:1, one launch (start us, length us, event | category | flops | bytes accessed | tf_op | source)
XLA Modules:
  0.0 52.0 jit_solution(13182058721109145849)
XLA Ops:
  0.6 50.4 %attention.1 = (f32[128,1536]{1,0:T(8,128)S(1)}, f32[128,1536]{1,0:T(8,128)S(1)}) custom-call(bf16[1,128,1536]{2,1,0:T(8,128)(2,1)} %q_hbm.1, bf16[1,128,1536]{2,1,0:T(8,128)(2,1)} %qt_hbm.1, bf16[1,128,1536]{2,1,0:T(8,128)(2,1)} %k_hbm.1, bf16[1,128,1536]{2,1,0:T(8,128)(2,1)} %kt_hbm.1, bf16[1,128,1536]{2,1,0:T(8,128)(2,1)} %v_hbm.1, ...), custom_call_target="tpu_custom_call" | custom-call | flops 7000000000 | bytes 10000000 | tf_op jit(solution)/shard_map/attention/pallas_call | solution.py:373
  51.1 1.0 %convert_bitcast_fusion = (bf16[1,128,1536]{2,1,0:T(8,128)(2,1)}, bf16[1,128,1536]{2,1,0:T(8,128)(2,1)}) fusion(f32[128,1536]{1,0:T(8,128)S(1)} %get-tuple-element.5, f32[128,1536]{1,0:T(8,128)S(1)} %get-tuple-element.4), kind=kLoop, calls=%fused_computation | loop fusion | flops 393216 | bytes 2359296 | tf_op jit(solution)/shard_map/broadcast_in_dim | solution.py:417
